TPU v7x, 256 devices: a whole 4x4x8 slice. The times are simulated.
256 devices in a mesh: seq: 8 (over x_hi, y), row: 32 (over x_lo, z, core).
Axes of the slice: x: 4 (x_hi: 2, x_lo: 2; x = x_hi * 2 + x_lo), y: 4, z: 8, core: 2. Of those that a mesh axis runs over, the one named last changes fastest.
Arguments:
- tokens: bfloat16 [2, 2048, 3072], P(None, ('seq', 'row')), may hold values from -6 to 6
- w_qkv: bfloat16 [6144, 3072], P('row'), may hold values from -0.109375 to 0.109375
- w_rate: bfloat16 [32, 3072], P('row'), may hold values from -0.109375 to 0.109375
- rate_bias: float32 [32], P('row'), may hold values from -3 to 1
- w_out: bfloat16 [2048, 3072], P('row'), may hold values from -0.125 to 0.125
- w_first_init: float32 [32, 64, 256], P('row'), may hold values from -0.75 to 0.75
- b_first_init: float32 [32, 256], P('row'), may hold values from -3 to 3
- w_second_init: float32 [32, 256, 64], P('row'), may hold values from -0.375 to 0.375
- b_second_init: float32 [32, 64], P('row'), may hold values from -3 to 3
- ln_gain: float32 [32, 64], P('row'), may hold values from 0.5 to 1.5
- ln_bias: float32 [32, 64], P('row'), may hold values from -3 to 3
Outputs:
- mixed: bfloat16 [2, 2048, 3072], P(None, ('seq', 'row'))
All inputs are finite; a program needn't handle non-finite values.
Results may differ from a plain program's by a relative error of at most 0.0056.
Values may be sent and summed in bfloat16 or wider, within the bound.
A program may use at most 64 MiB of HBM per device.

v0:
```python
from functools import partial
import jax
import jax.numpy as jnp
from jax import lax
from jax.sharding import PartitionSpec as P

MINI = 64
gelu_coef = 0.7978845608028654
base_rate = 0.01
ln_eps = 1e-06


def passed_along(array, axis, by):
    size = lax.axis_size(axis)
    pairs = [(i, i + by) for i in range(size) if 0 <= i + by < size]
    return lax.ppermute(array, axis, pairs)


def gelu_tanh(entries):
    tanh_arg = gelu_coef * (entries + 0.044715 * entries * entries * entries)
    return 0.5 * entries * (1.0 + jnp.tanh(tanh_arg))


def gelu_slope(entries):
    tanh_arg = gelu_coef * (entries + 0.044715 * entries * entries * entries)
    tangent = jnp.tanh(tanh_arg)
    return 0.5 * (1.0 + tangent) + 0.5 * entries * (1.0 - tangent * tangent) * gelu_coef * (
        1.0 + 3.0 * 0.044715 * entries * entries
    )


def matmul(left, right):
    return jnp.dot(left, right, precision=lax.Precision.HIGHEST, preferred_element_type=jnp.float32)


def normalize(entries):
    centred = entries - jnp.mean(entries, axis=-1, keepdims=True)
    spread = jnp.sqrt(jnp.mean(centred * centred, axis=-1, keepdims=True) + ln_eps)
    return (centred / spread, spread)


def mini_step(inner_state, batch_block, norm_gain, offset):
    w_first, b_first, w_second, b_second = inner_state
    queries, key_rows, value_rows, lr_rows = batch_block
    mini_len = queries.shape[0]
    hidden_pre = matmul(key_rows, w_first) + b_first
    hidden = gelu_tanh(hidden_pre)
    second = matmul(hidden, w_second) + b_second
    target = value_rows - key_rows
    normed, spread = normalize(second)
    grad_out = norm_gain * (norm_gain * normed + offset - target)
    feat_width = second.shape[-1]
    grad_second = (
        feat_width * grad_out
        - jnp.sum(grad_out, axis=-1, keepdims=True)
        - normed * jnp.sum(grad_out * normed, axis=-1, keepdims=True)
    ) / (feat_width * spread)
    grad_first = matmul(grad_second, w_second.T) * gelu_slope(hidden_pre)
    tri_mask = jnp.tril(jnp.ones((mini_len, mini_len), jnp.float32))
    eta_last = lr_rows / mini_len
    eta_table = tri_mask * eta_last[None, :]
    query_keys = matmul(queries, key_rows.T) * eta_table
    bias_first = b_first - matmul(eta_table, grad_first)
    first_bar = matmul(queries, w_first) - matmul(query_keys, grad_first) + bias_first
    hidden_bar = gelu_tanh(first_bar)
    hidden_pairs = matmul(hidden_bar, hidden.T) * eta_table
    bias_second = b_second - matmul(eta_table, grad_second)
    second_bar = matmul(hidden_bar, w_second) - matmul(hidden_pairs, grad_second) + bias_second
    w_first = w_first - matmul((key_rows * eta_last[:, None]).T, grad_first)
    b_first = b_first - matmul(eta_last[None, :], grad_first)[0]
    w_second = w_second - matmul((hidden * eta_last[:, None]).T, grad_second)
    b_second = b_second - matmul(eta_last[None, :], grad_second)[0]
    normed_bar, spread_bar = normalize(second_bar)
    result = queries + norm_gain * normed_bar + offset
    return ((w_first, b_first, w_second, b_second), result)


def run_blocks(inner_state, queries, key_rows, value_rows, lr_rows, norm_gain, offset, mini_len):
    block_count = queries.shape[0] // mini_len
    blocks = (
        queries.reshape(block_count, mini_len, -1),
        key_rows.reshape(block_count, mini_len, -1),
        value_rows.reshape(block_count, mini_len, -1),
        lr_rows.reshape(block_count, mini_len),
    )

    def advance(loop_carry, batch_block):
        return mini_step(loop_carry, batch_block, norm_gain, offset)

    inner_state, results = lax.scan(advance, inner_state, blocks)
    return (inner_state, results.reshape(queries.shape[0], -1))


def pack_state(state):
    videos = state[0].shape[0]
    return jnp.concatenate([part.reshape(videos, -1) for part in state], axis=1)


def unpack_state(flat, like):
    parts = []
    at = 0
    for part in like:
        width = part[0].size
        parts.append(flat[:, at : at + width].reshape(part.shape))
        at += width
    return tuple(parts)


def on_device(
    tokens,
    w_qkv,
    w_rate,
    rate_bias,
    w_out,
    w_first_init,
    b_first_init,
    w_second_init,
    b_second_init,
    ln_gain,
    ln_bias,
):
    videos, tok_part, feat_width = tokens.shape
    row_axes = ("xlo", "z", "core")
    pair_axes = ("xlo", "core")
    row_count = lax.axis_size(row_axes)
    z_count = lax.axis_size("z")
    pair_count = lax.axis_size(pair_axes)
    seg_len = tok_part * row_count
    proj_width = w_qkv.shape[0]
    head_size = proj_width // 3
    stacked = jnp.concatenate([w_qkv, w_rate], axis=0)
    gathered = lax.all_gather(tokens, row_axes, axis=1, tiled=True)
    gathered, w_out = lax.optimization_barrier((gathered, w_out))
    w_out_pair = lax.all_gather(w_out, pair_axes, axis=0, tiled=True)
    combined = jnp.einsum("vkd,cd->vkc", gathered, stacked, preferred_element_type=jnp.float32)
    projected = lax.optimization_barrier(combined[:, :, :proj_width].astype(jnp.bfloat16)).astype(
        jnp.float32
    )
    queries = projected[:, :, :head_size]
    key_rows = projected[:, :, head_size : 2 * head_size]
    value_rows = projected[:, :, 2 * head_size :]
    lr_rows = base_rate * jax.nn.sigmoid(combined[:, :, proj_width] + rate_bias[0])
    initial = (w_first_init[0], b_first_init[0], w_second_init[0], b_second_init[0])
    norm_gain = ln_gain[0]
    offset = ln_bias[0]

    def segment(inner_state, video_q, video_k, video_v, video_lr):
        return run_blocks(inner_state, video_q, video_k, video_v, video_lr, norm_gain, offset, MINI)

    seq_count = lax.axis_size("seq")
    seq_place = lax.axis_index("seq")
    first_device = seq_place == 0

    def spread_videos(entries):
        return jnp.broadcast_to(entries, (videos,) + entries.shape)

    start_states = jax.tree.map(spread_videos, initial)
    incoming = start_states
    for turn_idx in range(seq_count):
        finals, results = jax.vmap(segment)(incoming, queries, key_rows, value_rows, lr_rows)
        if turn_idx == 1:
            w_out_pair, finals = lax.optimization_barrier((w_out_pair, finals))
        if turn_idx + 1 < seq_count:
            with jax.named_scope("state_hop"):
                received = unpack_state(passed_along(pack_state(finals), "seq", 1), finals)
            incoming = jax.tree.map(partial(jnp.where, first_device), start_states, received)
    heads_rows = results.astype(jnp.bfloat16)
    with jax.named_scope("output_mix"):
        by_owner = heads_rows.reshape(videos, 2, z_count, 2, tok_part, head_size)
        by_owner = by_owner.transpose(1, 3, 0, 2, 4, 5).reshape(
            pair_count, videos, z_count, tok_part, head_size
        )
        by_head = lax.all_to_all(by_owner, pair_axes, 0, 0, tiled=True)
        partial_terms = jnp.einsum(
            "gvzic,gcd->zvid",
            by_head,
            w_out_pair.reshape(pair_count, head_size, feat_width),
            preferred_element_type=jnp.float32,
        )
        pieces = lax.all_to_all(partial_terms, "z", 0, 0, tiled=True)
        mixed_out = jnp.sum(pieces, axis=0)
    return mixed_out.reshape(videos, tok_part, feat_width).astype(jnp.bfloat16)


def solution(mesh):
    seq_count, row_count = mesh.devices.shape
    fine = jax.sharding.Mesh(
        mesh.devices.reshape(seq_count, 2, row_count // 4, 2), ("seq", "xlo", "z", "core")
    )
    row = ("xlo", "z", "core")
    in_specs = (
        P(None, ("seq",) + row, None),
        P(row, None),
        P(row, None),
        P(row),
        P(row, None),
        P(row, None, None),
        P(row, None),
        P(row, None, None),
        P(row, None),
        P(row, None),
        P(row, None),
    )
    out_specs = P(None, ("seq",) + row, None)
    return jax.shard_map(
        on_device, mesh=fine, in_specs=in_specs, out_specs=out_specs, check_vma=False
    )
```

profile of v0, /device:TPU:4, one launch (start us, length us, event | category | flops | bytes accessed | tf_op | source)
XLA Modules:
  0.0 341.9 jit_solution(8566038847159366962)
XLA Ops:
  6.5 0.7 all-gather.3.cloned.1.call-update
  7.9 70.0 %all-gather.3.cloned.1.call-done = bf16[2,256,3072]{2,1,0:T(8,128)(2,1)} async-done(((bf16[2,8,3072]{2,1,0:T(8,128)(2,1)}), bf16[2,256,3072]{2,1,0:T(8,128)(2,1)}) %all-gather.3.cloned.1.call-update) | async-done | bytes 3145744 | tf_op jit(solution)/shard_map/all_gather | solution.py:132
  78.0 3.4 fusion.200
  82.3 10.8 %while.130 = (s32[]{:T(128)}, f32[2,64,256]{2,1,0:T(8,128)S(1)}, f32[2,256]{1,0:T(2,128)S(1)}, f32[2,256,64]{1,2,0:T(8,128)S(1)}, f32[2,64]{1,0:T(2,128)S(1)}, /...) while((s32[]{:T(128)}, f32[2,64,256]{2,1,0:T(8,128)S(1)}, ...), condition=%wide.region_5.6_spmd, body=%wide.region_0.5_spmd.sunk | while | flops 127755136 | bytes 2386049 | solution.py:90
  84.3 0.4 convolution_subtract_fusion.38
  88.0 0.4 fusion.529
  89.6 0.4 convolution_subtract_fusion.38
  90.7 0.4 fusion.529
  92.3 0.4 convolution_subtract_fusion.38
  93.7 3.4 collective-permute-start
  97.2 10.5 %collective-permute-done = f32[2,33088]{1,0:T(2,128)S(1)} collective-permute-done((f32[2,33088]{1,0:T(2,128)S(1)}, f32[2,33088]{1,0:T(2,128)S(1)}, u32[]{:S(2)}, u32[]{:S(2)}) %collective-permute-start) | collective-permute-done | bytes 264736 | tf_op jit(solution)/shard_map/state_hop/ppermute | solution.py:16
  108.1 10.8 %while.131 = (s32[]{:T(128)}, f32[2,64,256]{2,1,0:T(8,128)S(1)}, f32[2,256]{1,0:T(2,128)S(1)}, f32[2,256,64]{1,2,0:T(8,128)S(1)}, f32[2,64]{1,0:T(2,128)S(1)}, /...) while((s32[]{:T(128)}, f32[2,64,256]{2,1,0:T(8,128)S(1)}, ...), condition=%wide.region_11.12_spmd, body=%wide.region_6.11_spmd.sunk | while | flops 127755136 | bytes 2386049 | solution.py:90
  108.4 0.4 fusion.546
  112.7 0.4 convolution_subtract_fusion.40
  113.8 0.4 fusion.546
  118.1 0.4 convolution_subtract_fusion.40
  118.9 5.2 %all-gather.5.cloned.1.call-done = bf16[256,3072]{1,0:T(8,128)(2,1)} async-done(((bf16[64,3072]{1,0:T(8,128)(2,1)}), bf16[256,3072]{1,0:T(8,128)(2,1)}) %all-gather.5.cloned.1.call-update) | async-done | bytes 1572880 | tf_op jit(solution)/shard_map/all_gather | solution.py:134
  124.7 3.3 collective-permute-start.1
  128.0 10.7 %collective-permute-done.1 = f32[2,33088]{1,0:T(2,128)S(1)} collective-permute-done((f32[2,33088]{1,0:T(2,128)S(1)}, f32[2,33088]{1,0:T(2,128)S(1)}, u32[]{:S(2)}, u32[]{:S(2)}) %collective-permute-start.1) | collective-permute-done | bytes 264736 | tf_op jit(solution)/shard_map/state_hop/ppermute | solution.py:16
  139.2 10.8 %while.132 = (s32[]{:T(128)}, f32[2,64,256]{2,1,0:T(8,128)S(1)}, f32[2,256]{1,0:T(2,128)S(1)}, f32[2,256,64]{1,2,0:T(8,128)S(1)}, f32[2,64]{1,0:T(2,128)S(1)}, /...) while((s32[]{:T(128)}, f32[2,64,256]{2,1,0:T(8,128)S(1)}, ...), condition=%wide.region_17.18_spmd, body=%wide.region_12.17_spmd.sunk | while | flops 127755136 | bytes 2386049 | solution.py:90
  139.5 0.4 fusion.563
  142.2 0.4 fusion.563
  143.8 0.4 convolution_subtract_fusion.42
  147.6 0.4 fusion.563
  149.2 0.4 convolution_subtract_fusion.42
  150.5 1.9 collective-permute-start.2
  152.5 11.4 %collective-permute-done.2 = f32[2,33088]{1,0:T(2,128)S(1)} collective-permute-done((f32[2,33088]{1,0:T(2,128)S(1)}, f32[2,33088]{1,0:T(2,128)S(1)}, u32[]{:S(2)}, u32[]{:S(2)}) %collective-permute-start.2) | collective-permute-done | bytes 264736 | tf_op jit(solution)/shard_map/state_hop/ppermute | solution.py:16
  164.2 10.8 %while.133 = (s32[]{:T(128)}, f32[2,64,256]{2,1,0:T(8,128)S(1)}, f32[2,256]{1,0:T(2,128)S(1)}, f32[2,256,64]{1,2,0:T(8,128)S(1)}, f32[2,64]{1,0:T(2,128)S(1)}, /...) while((s32[]{:T(128)}, f32[2,64,256]{2,1,0:T(8,128)S(1)}, ...), condition=%wide.region_23.24_spmd, body=%wide.region_18.23_spmd.sunk | while | flops 127755136 | bytes 2386049 | solution.py:90
  164.5 0.4 fusion.580
  167.2 0.4 fusion.580
  168.8 0.4 convolution_subtract_fusion.44
  172.6 0.4 fusion.580
  174.2 0.4 convolution_subtract_fusion.44
  175.6 2.1 collective-permute-start.3
  177.7 10.3 %collective-permute-done.3 = f32[2,33088]{1,0:T(2,128)S(1)} collective-permute-done((f32[2,33088]{1,0:T(2,128)S(1)}, f32[2,33088]{1,0:T(2,128)S(1)}, u32[]{:S(2)}, u32[]{:S(2)}) %collective-permute-start.3) | collective-permute-done | bytes 264736 | tf_op jit(solution)/shard_map/state_hop/ppermute | solution.py:16
  188.4 10.8 %while.134 = (s32[]{:T(128)}, f32[2,64,256]{2,1,0:T(8,128)S(1)}, f32[2,256]{1,0:T(2,128)S(1)}, f32[2,256,64]{1,2,0:T(8,128)S(1)}, f32[2,64]{1,0:T(2,128)S(1)}, /...) while((s32[]{:T(128)}, f32[2,64,256]{2,1,0:T(8,128)S(1)}, ...), condition=%wide.region_29.30_spmd, body=%wide.region_24.29_spmd.sunk | while | flops 127755136 | bytes 2386049 | solution.py:90
  191.3 0.4 fusion.597
  193.0 0.4 convolution_subtract_fusion.46
  196.7 0.4 fusion.597
  198.4 0.4 convolution_subtract_fusion.46
  199.7 1.9 collective-permute-start.4
  201.6 10.0 %collective-permute-done.4 = f32[2,33088]{1,0:T(2,128)S(1)} collective-permute-done((f32[2,33088]{1,0:T(2,128)S(1)}, f32[2,33088]{1,0:T(2,128)S(1)}, u32[]{:S(2)}, u32[]{:S(2)}) %collective-permute-start.4) | collective-permute-done | bytes 264736 | tf_op jit(solution)/shard_map/state_hop/ppermute | solution.py:16
  212.0 10.8 %while.135 = (s32[]{:T(128)}, f32[2,64,256]{2,1,0:T(8,128)S(1)}, f32[2,256]{1,0:T(2,128)S(1)}, f32[2,256,64]{1,2,0:T(8,128)S(1)}, f32[2,64]{1,0:T(2,128)S(1)}, /...) while((s32[]{:T(128)}, f32[2,64,256]{2,1,0:T(8,128)S(1)}, ...), condition=%wide.region_35.36_spmd, body=%wide.region_30.35_spmd.sunk | while | flops 127755136 | bytes 2386049 | solution.py:90
  215.0 0.4 fusion.614
  216.6 0.4 convolution_subtract_fusion.48
  220.4 0.4 fusion.614
  222.1 0.4 convolution_subtract_fusion.48
  223.4 1.9 collective-permute-start.5
  225.3 10.0 %collective-permute-done.5 = f32[2,33088]{1,0:T(2,128)S(1)} collective-permute-done((f32[2,33088]{1,0:T(2,128)S(1)}, f32[2,33088]{1,0:T(2,128)S(1)}, u32[]{:S(2)}, u32[]{:S(2)}) %collective-permute-start.5) | collective-permute-done | bytes 264736 | tf_op jit(solution)/shard_map/state_hop/ppermute | solution.py:16
  235.7 10.8 %while.136 = (s32[]{:T(128)}, f32[2,64,256]{2,1,0:T(8,128)S(1)}, f32[2,256]{1,0:T(2,128)S(1)}, f32[2,256,64]{1,2,0:T(8,128)S(1)}, f32[2,64]{1,0:T(2,128)S(1)}, /...) while((s32[]{:T(128)}, f32[2,64,256]{2,1,0:T(8,128)S(1)}, ...), condition=%wide.region_41.42_spmd, body=%wide.region_36.41_spmd.sunk | while | flops 127755136 | bytes 2386049 | solution.py:90
  240.3 0.4 convolution_subtract_fusion.50
  245.7 0.4 convolution_subtract_fusion.50
  247.1 1.9 collective-permute-start.6
  249.3 9.7 %collective-permute-done.6 = f32[2,33088]{1,0:T(2,128)S(1)} collective-permute-done((f32[2,33088]{1,0:T(2,128)S(1)}, f32[2,33088]{1,0:T(2,128)S(1)}, u32[]{:S(2)}, u32[]{:S(2)}) %collective-permute-start.6) | collective-permute-done | bytes 264736 | tf_op jit(solution)/shard_map/state_hop/ppermute | solution.py:16
  259.4 20.8 %while.137 = (s32[]{:T(128)}, f32[2,64,256]{2,1,0:T(8,128)S(1)}, f32[2,256]{1,0:T(2,128)S(1)}, f32[2,256,64]{1,2,0:T(8,128)S(1)}, f32[2,64]{1,0:T(2,128)S(1)}, /...) while((s32[]{:T(128)}, f32[2,64,256]{2,1,0:T(8,128)S(1)}, ...), condition=%wide.region_49.50_spmd, body=%wide.region_42.49_spmd.sunk | while | flops 273236992 | bytes 4856473 | solution.py:90
  263.8 0.4 convolution_subtract_fusion.52
  269.0 0.4 convolution_subtract_fusion.52
  270.1 0.4 fusion.662
  275.3 0.4 fusion.662
  279.4 0.4 convolution_subtract_fusion.52
  280.4 6.5 %all_to_all.10 = bf16[4,2,4096]{2,1,0:T(2,128)(2,1)S(1)} all-to-all(bf16[4,2,4096]{2,1,0:T(2,128)(2,1)S(1)} %reshape.525), channel_id=1, replica_groups=mesh['seq'=8,'xlo'=2,'z'=8,'core'=2] {'xlo','core'}, dimensions={0} | all-to-all | bytes 131072 | tf_op jit(solution)/shard_map/output_mix/all_to_all | solution.py:173
  287.1 0.4 convolution_bitcast_fusion
  287.6 46.7 %all_to_all.11 = f32[8,2,8,3072]{3,2,1,0:T(8,128)S(1)} all-to-all(f32[8,2,8,3072]{3,2,1,0:T(8,128)S(1)} %copy.214), channel_id=1, replica_groups=mesh['seq'=8,'xlo'=2,'z'=8,'core'=2] {'z'}, dimensions={0} | all-to-all | bytes 3145728 | tf_op jit(solution)/shard_map/output_mix/all_to_all | solution.py:180
  334.3 0.7 reduce_sum.315
  (645 shorter events, 88.1 us)
Async XLA Ops:
  6.5 71.4 %all-gather.3.cloned.1.call-start = ((), (), s32[]{:S(2)}) async-start(), calls=%async_computation.2 | async-start | bytes 3244032 | tf_op jit(solution)/shard_map/all_gather | solution.py:132
  7.3 116.9 %all-gather.5.cloned.1.call-start = ((), (), s32[]{:S(2)}) async-start(), calls=%async_computation.3 | async-start | bytes 1966080 | tf_op jit(solution)/shard_map/all_gather | solution.py:134
  81.4 0.9 copy-start
  81.4 0.9 copy-start.4
  81.4 0.9 copy-start.5
  81.4 0.9 copy-start.3
  81.4 0.9 copy-start.1
  81.4 0.9 copy-start.2
  93.7 14.0 %collective-permute-start = (f32[2,33088]{1,0:T(2,128)S(1)}, f32[2,33088]{1,0:T(2,128)S(1)}, u32[]{:S(2)}, u32[]{:S(2)}) collective-permute-start(f32[2,33088]{1,0:T(2,128)S(1)} %pad_maximum_fusion), channel_id=1, source_target_pairs={{0,32},{32,64},{64,96},{96,128},{128,160},{160,192},{192,224},{1,3... | collective-permute-start | bytes 794120 | tf_op jit(solution)/shard_map/state_hop/ppermute | solution.py:16
  124.7 14.1 %collective-permute-start.1 = (f32[2,33088]{1,0:T(2,128)S(1)}, f32[2,33088]{1,0:T(2,128)S(1)}, u32[]{:S(2)}, u32[]{:S(2)}) collective-permute-start(f32[2,33088]{1,0:T(2,128)S(1)} %pad_maximum_fusion.1), channel_id=1, source_target_pairs={{0,32},{32,64},{64,96},{96,128},{128,160},{160,192},{192,224},{1,3... | collective-permute-start | bytes 794120 | tf_op jit(solution)/shard_map/state_hop/ppermute | solution.py:16
  150.5 13.3 %collective-permute-start.2 = (f32[2,33088]{1,0:T(2,128)S(1)}, f32[2,33088]{1,0:T(2,128)S(1)}, u32[]{:S(2)}, u32[]{:S(2)}) collective-permute-start(f32[2,33088]{1,0:T(2,128)S(1)} %pad_maximum_fusion.2), channel_id=1, source_target_pairs={{0,32},{32,64},{64,96},{96,128},{128,160},{160,192},{192,224},{1,3... | collective-permute-start | bytes 794120 | tf_op jit(solution)/shard_map/state_hop/ppermute | solution.py:16
  175.6 12.4 %collective-permute-start.3 = (f32[2,33088]{1,0:T(2,128)S(1)}, f32[2,33088]{1,0:T(2,128)S(1)}, u32[]{:S(2)}, u32[]{:S(2)}) collective-permute-start(f32[2,33088]{1,0:T(2,128)S(1)} %pad_maximum_fusion.3), channel_id=1, source_target_pairs={{0,32},{32,64},{64,96},{96,128},{128,160},{160,192},{192,224},{1,3... | collective-permute-start | bytes 794120 | tf_op jit(solution)/shard_map/state_hop/ppermute | solution.py:16
  199.7 11.9 %collective-permute-start.4 = (f32[2,33088]{1,0:T(2,128)S(1)}, f32[2,33088]{1,0:T(2,128)S(1)}, u32[]{:S(2)}, u32[]{:S(2)}) collective-permute-start(f32[2,33088]{1,0:T(2,128)S(1)} %pad_maximum_fusion.4), channel_id=1, source_target_pairs={{0,32},{32,64},{64,96},{96,128},{128,160},{160,192},{192,224},{1,3... | collective-permute-start | bytes 794120 | tf_op jit(solution)/shard_map/state_hop/ppermute | solution.py:16
  223.4 11.9 %collective-permute-start.5 = (f32[2,33088]{1,0:T(2,128)S(1)}, f32[2,33088]{1,0:T(2,128)S(1)}, u32[]{:S(2)}, u32[]{:S(2)}) collective-permute-start(f32[2,33088]{1,0:T(2,128)S(1)} %pad_maximum_fusion.5), channel_id=1, source_target_pairs={{0,32},{32,64},{64,96},{96,128},{128,160},{160,192},{192,224},{1,3... | collective-permute-start | bytes 794120 | tf_op jit(solution)/shard_map/state_hop/ppermute | solution.py:16
  247.1 11.9 %collective-permute-start.6 = (f32[2,33088]{1,0:T(2,128)S(1)}, f32[2,33088]{1,0:T(2,128)S(1)}, u32[]{:S(2)}, u32[]{:S(2)}) collective-permute-start(f32[2,33088]{1,0:T(2,128)S(1)} %pad_maximum_fusion.6), channel_id=1, source_target_pairs={{0,32},{32,64},{64,96},{96,128},{128,160},{160,192},{192,224},{1,3... | collective-permute-start | bytes 794120 | tf_op jit(solution)/shard_map/state_hop/ppermute | solution.py:16
  259.4 27.6 %copy-start.6 = (bf16[256,3072]{1,0:T(8,128)(2,1)S(1)}, bf16[256,3072]{1,0:T(8,128)(2,1)}, u32[]{:S(2)}) copy-start(bf16[256,3072]{1,0:T(8,128)(2,1)} %all-gather.5.cloned.1.call-done) | copy-start | bytes 4718596
Sparse Core Ops, SparseCore 0:
  9.2 68.7 all-gather.2
  97.3 26.7 all-gather.4
where the time goes:
time: 342 us
  waiting for transfers between devices  148 us (43%)
  matrix products  77.1 us (23%)
  blocking collectives  53.2 us (16%)
  other arithmetic  22.5 us (7%)
  starting transfers between devices  16.6 us (5%)
  between operations  14.9 us (4%)
  local copies, waits for them, and re-layouts  6.66 us (2%)
    dot_general x256, matrix products, matmul(): jnp.dot(left, right, precision=lax.Precision.HIGHEST, preferred_element_t...  73.3 us
    ppermute x7, waiting for transfers between devices, passed_along(): return lax.ppermute(array, axis, pairs)  72.5 us
    all_gather x1, waiting for transfers between devices, on_device(): gathered = lax.all_gather(tokens, row_axes, axis=1, tiled=True)  70 us
    all_to_all x1, blocking collectives, on_device(): pieces = lax.all_to_all(partial_terms, 'z', 0, 0, tiled=True)  46.7 us
    ppermute x7, starting transfers between devices, passed_along(): return lax.ppermute(array, axis, pairs)  16.5 us
    reduce_sum x32, other arithmetic, mini_step(): jnp.sum(grad_out, axis=-1, keepdims=True)  6.92 us
  transfers between devices with their start and end apart: 9, of which 9 were waited for; matrix products, arithmetic and copies ran while one was open for 3% of the time, Pallas kernels for 0%

commit v1 on v0

--- a/solution.py
+++ b/solution.py
@@ -129,7 +129,9 @@
     proj_width = w_qkv.shape[0]
     head_size = proj_width // 3
     stacked = jnp.concatenate([w_qkv, w_rate], axis=0)
-    gathered = lax.all_gather(tokens, row_axes, axis=1, tiled=True)
+    gathered = jnp.concatenate(
+        lax.all_to_all(jnp.stack([tokens] * lax.axis_size(row_axes)), row_axes, 0, 0), axis=1
+    )
     gathered, w_out = lax.optimization_barrier((gathered, w_out))
     w_out_pair = lax.all_gather(w_out, pair_axes, axis=0, tiled=True)
     combined = jnp.einsum("vkd,cd->vkc", gathered, stacked, preferred_element_type=jnp.float32)

time: 342 us -> 356 us (1.041)
  starting transfers between devices: 16.6 us -> 26.6 us
  local copies, waits for them, and re-layouts: 6.66 us -> 10.8 us
    all_to_all x0 -> x1, waiting for transfers between devices: none -> 72.1 us  [on_device(): lax.all_to_all(jnp.stack([tokens] * lax.axis_size(row_axes)), row_axes, 0...]
    all_gather x1 -> x0, waiting for transfers between devices: 70 us -> none  [on_device(): gathered = lax.all_gather(tokens, row_axes, axis=1, tiled=True)]
    all_to_all x0 -> x1, starting transfers between devices: none -> 9.49 us  [on_device(): lax.all_to_all(jnp.stack([tokens] * lax.axis_size(row_axes)), row_axes, 0...]
where the time goes in v1:
time: 356 us
  waiting for transfers between devices  149 us (42%)
  matrix products  76.3 us (21%)
  blocking collectives  53.2 us (15%)
  starting transfers between devices  26.6 us (7%)
  other arithmetic  22.4 us (6%)
  between operations  14.9 us (4%)
  local copies, waits for them, and re-layouts  10.8 us (3%)
    dot_general x256, matrix products, matmul(): jnp.dot(left, right, precision=lax.Precision.HIGHEST, preferred_element_t...  73.3 us
    all_to_all x1, waiting for transfers between devices, on_device(): lax.all_to_all(jnp.stack([tokens] * lax.axis_size(row_axes)), row_axes, 0...  72.1 us
    ppermute x7, waiting for transfers between devices, passed_along(): return lax.ppermute(array, axis, pairs)  71.2 us
    all_to_all x1, blocking collectives, on_device(): pieces = lax.all_to_all(partial_terms, 'z', 0, 0, tiled=True)  46.7 us
    ppermute x7, starting transfers between devices, passed_along(): return lax.ppermute(array, axis, pairs)  17.1 us
    all_to_all x1, starting transfers between devices, on_device(): lax.all_to_all(jnp.stack([tokens] * lax.axis_size(row_axes)), row_axes, 0...  9.49 us
  transfers between devices with their start and end apart: 9, of which 9 were waited for; matrix products, arithmetic and copies ran while one was open for 3% of the time, Pallas kernels for 0%

profile of v1, /device:TPU:4, one launch (start us, length us, event | category | flops | bytes accessed | tf_op | source)
XLA Modules:
  0.0 355.5 jit_solution(7537193446403550508)
XLA Ops:
  6.5 2.9 stack.2
  9.5 9.5 %all-to-all-start = ((bf16[32,2,8,3072]{3,2,1,0:T(8,128)(2,1)}), bf16[32,2,8,3072]{3,2,1,0:T(8,128)(2,1)S(1)}, u32[]{:S(2)}, u32[]{:S(2)}) async-start(bf16[32,2,8,3072]{3,2,1,0:T(8,128)(2,1)} %stack.2), calls=%async_computation | async-start | bytes 6291456 | tf_op jit(solution)/shard_map/all_to_all | solution.py:133
  19.7 72.1 %all-to-all-done = bf16[32,2,8,3072]{3,2,1,0:T(8,128)(2,1)S(1)} async-done(((bf16[32,2,8,3072]{3,2,1,0:T(8,128)(2,1)}), bf16[32,2,8,3072]{3,2,1,0:T(8,128)(2,1)S(1)}, u32[]{:S(2)}, u32[]{:S(2)}) %all-to-all-start) | async-done | bytes 3145760 | tf_op jit(solution)/shard_map/all_to_all | solution.py:133
  92.0 1.0 copy-done.6
  93.0 1.2 fusion.200
  95.2 10.8 %while.130 = (s32[]{:T(128)}, f32[2,64,256]{2,1,0:T(8,128)S(1)}, f32[2,256]{1,0:T(2,128)S(1)}, f32[2,256,64]{1,2,0:T(8,128)S(1)}, f32[2,64]{1,0:T(2,128)S(1)}, /...) while((s32[]{:T(128)}, f32[2,64,256]{2,1,0:T(8,128)S(1)}, ...), condition=%wide.region_5.6_spmd, body=%wide.region_0.5_spmd.sunk | while | flops 127755136 | bytes 2386049 | solution.py:90
  95.5 0.4 fusion.529
  97.1 0.4 convolution_subtract_fusion.38
  98.2 0.4 fusion.529
  99.8 0.4 convolution_subtract_fusion.38
  102.5 0.4 convolution_subtract_fusion.38
  103.6 0.4 fusion.529
  105.2 0.4 convolution_subtract_fusion.38
  106.5 3.5 collective-permute-start
  110.2 9.8 %collective-permute-done = f32[2,33088]{1,0:T(2,128)S(1)} collective-permute-done((f32[2,33088]{1,0:T(2,128)S(1)}, f32[2,33088]{1,0:T(2,128)S(1)}, u32[]{:S(2)}, u32[]{:S(2)}) %collective-permute-start) | collective-permute-done | bytes 264736 | tf_op jit(solution)/shard_map/state_hop/ppermute | solution.py:16
  120.3 10.8 %while.131 = (s32[]{:T(128)}, f32[2,64,256]{2,1,0:T(8,128)S(1)}, f32[2,256]{1,0:T(2,128)S(1)}, f32[2,256,64]{1,2,0:T(8,128)S(1)}, f32[2,64]{1,0:T(2,128)S(1)}, /...) while((s32[]{:T(128)}, f32[2,64,256]{2,1,0:T(8,128)S(1)}, ...), condition=%wide.region_11.12_spmd, body=%wide.region_6.11_spmd.sunk | while | flops 127755136 | bytes 2386049 | solution.py:90
  122.2 0.4 convolution_subtract_fusion.40
  124.9 0.4 convolution_subtract_fusion.40
  127.6 0.4 convolution_subtract_fusion.40
  130.3 0.4 convolution_subtract_fusion.40
  131.1 5.3 %all-gather.2.cloned.1.call-done = bf16[256,3072]{1,0:T(8,128)(2,1)} async-done(((bf16[64,3072]{1,0:T(8,128)(2,1)}), bf16[256,3072]{1,0:T(8,128)(2,1)}) %all-gather.2.cloned.1.call-update) | async-done | bytes 1572880 | tf_op jit(solution)/shard_map/all_gather | solution.py:136
  137.0 3.6 %collective-permute-start.1 = (f32[2,33088]{1,0:T(2,128)S(1)}, f32[2,33088]{1,0:T(2,128)S(1)}, u32[]{:S(2)}, u32[]{:S(2)}) collective-permute-start(f32[2,33088]{1,0:T(2,128)S(1)} %pad_maximum_fusion.1), channel_id=1, source_target_pairs={{0,32},{32,64},{64,96},{96,128},{128,160},{160,192},{192,224},{1,3... | collective-permute-start | bytes 794120 | tf_op jit(solution)/shard_map/state_hop/ppermute | solution.py:16
  140.6 10.5 %collective-permute-done.1 = f32[2,33088]{1,0:T(2,128)S(1)} collective-permute-done((f32[2,33088]{1,0:T(2,128)S(1)}, f32[2,33088]{1,0:T(2,128)S(1)}, u32[]{:S(2)}, u32[]{:S(2)}) %collective-permute-start.1) | collective-permute-done | bytes 264736 | tf_op jit(solution)/shard_map/state_hop/ppermute | solution.py:16
  151.5 10.8 %while.132 = (s32[]{:T(128)}, f32[2,64,256]{2,1,0:T(8,128)S(1)}, f32[2,256]{1,0:T(2,128)S(1)}, f32[2,256,64]{1,2,0:T(8,128)S(1)}, f32[2,64]{1,0:T(2,128)S(1)}, /...) while((s32[]{:T(128)}, f32[2,64,256]{2,1,0:T(8,128)S(1)}, ...), condition=%wide.region_17.18_spmd, body=%wide.region_12.17_spmd.sunk | while | flops 127755136 | bytes 2386049 | solution.py:90
  151.8 0.4 fusion.563
  153.4 0.4 convolution_subtract_fusion.42
  156.1 0.4 convolution_subtract_fusion.42
  158.8 0.4 convolution_subtract_fusion.42
  161.5 0.4 convolution_subtract_fusion.42
  162.8 2.1 collective-permute-start.2
  164.9 11.2 %collective-permute-done.2 = f32[2,33088]{1,0:T(2,128)S(1)} collective-permute-done((f32[2,33088]{1,0:T(2,128)S(1)}, f32[2,33088]{1,0:T(2,128)S(1)}, u32[]{:S(2)}, u32[]{:S(2)}) %collective-permute-start.2) | collective-permute-done | bytes 264736 | tf_op jit(solution)/shard_map/state_hop/ppermute | solution.py:16
  176.5 10.8 %while.133 = (s32[]{:T(128)}, f32[2,64,256]{2,1,0:T(8,128)S(1)}, f32[2,256]{1,0:T(2,128)S(1)}, f32[2,256,64]{1,2,0:T(8,128)S(1)}, f32[2,64]{1,0:T(2,128)S(1)}, /...) while((s32[]{:T(128)}, f32[2,64,256]{2,1,0:T(8,128)S(1)}, ...), condition=%wide.region_23.24_spmd, body=%wide.region_18.23_spmd.sunk | while | flops 127755136 | bytes 2386049 | solution.py:90
  178.4 0.4 convolution_subtract_fusion.44
  181.1 0.4 convolution_subtract_fusion.44
  183.8 0.4 convolution_subtract_fusion.44
  186.5 0.4 convolution_subtract_fusion.44
  187.9 1.9 collective-permute-start.3
  189.8 10.4 %collective-permute-done.3 = f32[2,33088]{1,0:T(2,128)S(1)} collective-permute-done((f32[2,33088]{1,0:T(2,128)S(1)}, f32[2,33088]{1,0:T(2,128)S(1)}, u32[]{:S(2)}, u32[]{:S(2)}) %collective-permute-start.3) | collective-permute-done | bytes 264736 | tf_op jit(solution)/shard_map/state_hop/ppermute | solution.py:16
  200.6 10.8 %while.134 = (s32[]{:T(128)}, f32[2,64,256]{2,1,0:T(8,128)S(1)}, f32[2,256]{1,0:T(2,128)S(1)}, f32[2,256,64]{1,2,0:T(8,128)S(1)}, f32[2,64]{1,0:T(2,128)S(1)}, /...) while((s32[]{:T(128)}, f32[2,64,256]{2,1,0:T(8,128)S(1)}, ...), condition=%wide.region_29.30_spmd, body=%wide.region_24.29_spmd.sunk | while | flops 127755136 | bytes 2386049 | solution.py:90
  202.6 0.4 convolution_subtract_fusion.46
  205.2 0.4 convolution_subtract_fusion.46
  207.9 0.4 convolution_subtract_fusion.46
  210.7 0.4 convolution_subtract_fusion.46
  212.0 1.9 collective-permute-start.4
  213.9 10.0 %collective-permute-done.4 = f32[2,33088]{1,0:T(2,128)S(1)} collective-permute-done((f32[2,33088]{1,0:T(2,128)S(1)}, f32[2,33088]{1,0:T(2,128)S(1)}, u32[]{:S(2)}, u32[]{:S(2)}) %collective-permute-start.4) | collective-permute-done | bytes 264736 | tf_op jit(solution)/shard_map/state_hop/ppermute | solution.py:16
  224.3 10.8 %while.135 = (s32[]{:T(128)}, f32[2,64,256]{2,1,0:T(8,128)S(1)}, f32[2,256]{1,0:T(2,128)S(1)}, f32[2,256,64]{1,2,0:T(8,128)S(1)}, f32[2,64]{1,0:T(2,128)S(1)}, /...) while((s32[]{:T(128)}, f32[2,64,256]{2,1,0:T(8,128)S(1)}, ...), condition=%wide.region_35.36_spmd, body=%wide.region_30.35_spmd.sunk | while | flops 127755136 | bytes 2386049 | solution.py:90
  226.2 0.4 convolution_subtract_fusion.48
  228.9 0.4 convolution_subtract_fusion.48
  231.6 0.4 convolution_subtract_fusion.48
  234.3 0.4 convolution_subtract_fusion.48
  235.7 1.9 collective-permute-start.5
  237.6 10.0 %collective-permute-done.5 = f32[2,33088]{1,0:T(2,128)S(1)} collective-permute-done((f32[2,33088]{1,0:T(2,128)S(1)}, f32[2,33088]{1,0:T(2,128)S(1)}, u32[]{:S(2)}, u32[]{:S(2)}) %collective-permute-start.5) | collective-permute-done | bytes 264736 | tf_op jit(solution)/shard_map/state_hop/ppermute | solution.py:16
  248.0 10.8 %while.136 = (s32[]{:T(128)}, f32[2,64,256]{2,1,0:T(8,128)S(1)}, f32[2,256]{1,0:T(2,128)S(1)}, f32[2,256,64]{1,2,0:T(8,128)S(1)}, f32[2,64]{1,0:T(2,128)S(1)}, /...) while((s32[]{:T(128)}, f32[2,64,256]{2,1,0:T(8,128)S(1)}, ...), condition=%wide.region_41.42_spmd, body=%wide.region_36.41_spmd.sunk | while | flops 127755136 | bytes 2386049 | solution.py:90
  249.9 0.4 convolution_subtract_fusion.50
  252.6 0.4 convolution_subtract_fusion.50
  255.3 0.4 convolution_subtract_fusion.50
  258.0 0.4 convolution_subtract_fusion.50
  259.3 2.1 collective-permute-start.6
  261.8 9.4 %collective-permute-done.6 = f32[2,33088]{1,0:T(2,128)S(1)} collective-permute-done((f32[2,33088]{1,0:T(2,128)S(1)}, f32[2,33088]{1,0:T(2,128)S(1)}, u32[]{:S(2)}, u32[]{:S(2)}) %collective-permute-start.6) | collective-permute-done | bytes 264736 | tf_op jit(solution)/shard_map/state_hop/ppermute | solution.py:16
  271.7 20.8 %while.137 = (s32[]{:T(128)}, f32[2,64,256]{2,1,0:T(8,128)S(1)}, f32[2,256]{1,0:T(2,128)S(1)}, f32[2,256,64]{1,2,0:T(8,128)S(1)}, f32[2,64]{1,0:T(2,128)S(1)}, /...) while((s32[]{:T(128)}, f32[2,64,256]{2,1,0:T(8,128)S(1)}, ...), condition=%wide.region_49.50_spmd, body=%wide.region_42.49_spmd.sunk | while | flops 273236992 | bytes 4856473 | solution.py:90
  292.6 6.5 %all_to_all.15 = bf16[4,2,4096]{2,1,0:T(2,128)(2,1)S(1)} all-to-all(bf16[4,2,4096]{2,1,0:T(2,128)(2,1)S(1)} %reshape.535), channel_id=1, replica_groups=mesh['seq'=8,'xlo'=2,'z'=8,'core'=2] {'xlo','core'}, dimensions={0} | all-to-all | bytes 131072 | tf_op jit(solution)/shard_map/output_mix/all_to_all | solution.py:175
  299.3 1.8 convolution_bitcast_fusion
  301.3 46.7 %all_to_all.16 = f32[8,2,8,3072]{3,2,1,0:T(8,128)S(1)} all-to-all(f32[8,2,8,3072]{3,2,1,0:T(8,128)S(1)} %copy.215), channel_id=1, replica_groups=mesh['seq'=8,'xlo'=2,'z'=8,'core'=2] {'z'}, dimensions={0} | all-to-all | bytes 3145728 | tf_op jit(solution)/shard_map/output_mix/all_to_all | solution.py:182
  348.0 0.7 reduce_sum.315
  (648 shorter events, 89.0 us)
Async XLA Ops:
  9.5 82.3 %all-to-all-start = ((bf16[32,2,8,3072]{3,2,1,0:T(8,128)(2,1)}), bf16[32,2,8,3072]{3,2,1,0:T(8,128)(2,1)S(1)}, u32[]{:S(2)}, u32[]{:S(2)}) async-start(bf16[32,2,8,3072]{3,2,1,0:T(8,128)(2,1)} %stack.2), calls=%async_computation | async-start | bytes 6291456 | tf_op jit(solution)/shard_map/all_to_all | solution.py:133
  19.0 117.5 %all-gather.2.cloned.1.call-start = ((), (), s32[]{:S(2)}) async-start(), calls=%async_computation.3 | async-start | bytes 1966080 | tf_op jit(solution)/shard_map/all_gather | solution.py:136
  19.7 72.3 %copy-start.7 = (bf16[1,3072]{1,0:T(2,128)(2,1)S(1)}, bf16[1,3072]{1,0:T(2,128)(2,1)}, u32[]{:S(2)}) copy-start(bf16[1,3072]{1,0:T(2,128)(2,1)} %param.29) | copy-start | bytes 18436
  91.8 1.3 copy-start.6
  94.2 0.9 copy-start
  94.2 0.9 copy-start.4
  94.2 0.9 copy-start.5
  94.2 0.9 copy-start.3
  94.3 0.9 copy-start.1
  94.3 0.9 copy-start.2
  106.5 13.4 %collective-permute-start = (f32[2,33088]{1,0:T(2,128)S(1)}, f32[2,33088]{1,0:T(2,128)S(1)}, u32[]{:S(2)}, u32[]{:S(2)}) collective-permute-start(f32[2,33088]{1,0:T(2,128)S(1)} %pad_maximum_fusion), channel_id=1, source_target_pairs={{0,32},{32,64},{64,96},{96,128},{128,160},{160,192},{192,224},{1,3... | collective-permute-start | bytes 794120 | tf_op jit(solution)/shard_map/state_hop/ppermute | solution.py:16
  137.0 14.1 %collective-permute-start.1 = (f32[2,33088]{1,0:T(2,128)S(1)}, f32[2,33088]{1,0:T(2,128)S(1)}, u32[]{:S(2)}, u32[]{:S(2)}) collective-permute-start(f32[2,33088]{1,0:T(2,128)S(1)} %pad_maximum_fusion.1), channel_id=1, source_target_pairs={{0,32},{32,64},{64,96},{96,128},{128,160},{160,192},{192,224},{1,3... | collective-permute-start | bytes 794120 | tf_op jit(solution)/shard_map/state_hop/ppermute | solution.py:16
  162.8 13.3 %collective-permute-start.2 = (f32[2,33088]{1,0:T(2,128)S(1)}, f32[2,33088]{1,0:T(2,128)S(1)}, u32[]{:S(2)}, u32[]{:S(2)}) collective-permute-start(f32[2,33088]{1,0:T(2,128)S(1)} %pad_maximum_fusion.2), channel_id=1, source_target_pairs={{0,32},{32,64},{64,96},{96,128},{128,160},{160,192},{192,224},{1,3... | collective-permute-start | bytes 794120 | tf_op jit(solution)/shard_map/state_hop/ppermute | solution.py:16
  187.9 12.4 %collective-permute-start.3 = (f32[2,33088]{1,0:T(2,128)S(1)}, f32[2,33088]{1,0:T(2,128)S(1)}, u32[]{:S(2)}, u32[]{:S(2)}) collective-permute-start(f32[2,33088]{1,0:T(2,128)S(1)} %pad_maximum_fusion.3), channel_id=1, source_target_pairs={{0,32},{32,64},{64,96},{96,128},{128,160},{160,192},{192,224},{1,3... | collective-permute-start | bytes 794120 | tf_op jit(solution)/shard_map/state_hop/ppermute | solution.py:16
  212.0 11.9 %collective-permute-start.4 = (f32[2,33088]{1,0:T(2,128)S(1)}, f32[2,33088]{1,0:T(2,128)S(1)}, u32[]{:S(2)}, u32[]{:S(2)}) collective-permute-start(f32[2,33088]{1,0:T(2,128)S(1)} %pad_maximum_fusion.4), channel_id=1, source_target_pairs={{0,32},{32,64},{64,96},{96,128},{128,160},{160,192},{192,224},{1,3... | collective-permute-start | bytes 794120 | tf_op jit(solution)/shard_map/state_hop/ppermute | solution.py:16
  235.7 11.9 %collective-permute-start.5 = (f32[2,33088]{1,0:T(2,128)S(1)}, f32[2,33088]{1,0:T(2,128)S(1)}, u32[]{:S(2)}, u32[]{:S(2)}) collective-permute-start(f32[2,33088]{1,0:T(2,128)S(1)} %pad_maximum_fusion.5), channel_id=1, source_target_pairs={{0,32},{32,64},{64,96},{96,128},{128,160},{160,192},{192,224},{1,3... | collective-permute-start | bytes 794120 | tf_op jit(solution)/shard_map/state_hop/ppermute | solution.py:16
  259.3 11.9 %collective-permute-start.6 = (f32[2,33088]{1,0:T(2,128)S(1)}, f32[2,33088]{1,0:T(2,128)S(1)}, u32[]{:S(2)}, u32[]{:S(2)}) collective-permute-start(f32[2,33088]{1,0:T(2,128)S(1)} %pad_maximum_fusion.6), channel_id=1, source_target_pairs={{0,32},{32,64},{64,96},{96,128},{128,160},{160,192},{192,224},{1,3... | collective-permute-start | bytes 794120 | tf_op jit(solution)/shard_map/state_hop/ppermute | solution.py:16
Sparse Core Ops, SparseCore 0:
  110.3 26.1 all-gather.1
